TPU v7x, 512 devices: a whole 4x4x16 slice. The times are simulated.
512 devices in a mesh: dp: 8 (over x, z_hi), wide: 64 (over y, z_lo, core).
Axes of the slice: x: 4, y: 4, z: 16 (z_hi: 2, z_lo: 8; z = z_hi * 8 + z_lo), core: 2. Of those that a mesh axis runs over, the one named last changes fastest.
Arguments:
- latents: bfloat16 [8, 128, 8, 16, 256], P('dp', 'wide'), may hold values from -36 to 36
- cotangent: bfloat16 [8, 128, 8, 16, 256], P('dp', 'wide'), may hold values from -41 to 41
- norm_gain: float32 [256], replicated, may hold values from 0.25 to 1.75
- norm_bias: float32 [256], replicated, may hold values from -3 to 3
- w_spatial: bfloat16 [2304, 256], P('dp'), may hold values from -0.125 to 0.125
- w_temporal: bfloat16 [768, 256], P('dp'), may hold values from -0.21875 to 0.21875
Outputs:
- block_out: bfloat16 [8, 128, 8, 16, 256], P('dp', 'wide')
- grad_latents: bfloat16 [8, 128, 8, 16, 256], P('dp', 'wide')
- grad_spatial: float32 [2304, 256], P('dp', 'wide')
- grad_temporal: float32 [768, 256], P('dp', 'wide')
- grad_norm: float32 [2, 256], P(None, 'wide')
All inputs are finite; a program needn't handle non-finite values.
Results may differ from a plain program's by a relative error of at most 0.012.
Values may be sent and summed in bfloat16 or wider, within the bound.
A program may use at most 64 MiB of HBM per device.

v0:
```python
import math
import jax
import jax.numpy as jnp
from jax import lax
from jax.sharding import PartitionSpec as P

GROUPS = 32
epsilon = 1e-05


def contract(left, right):
    return lax.dot_general(
        left, right, (((0,), (0,)), ((), ())), preferred_element_type=jnp.float32
    )


def spatial_forward(activated, weights):
    frames, rows_here, cols_here, channels = activated.shape
    padded = jnp.pad(activated, ((0, 0), (1, 1), (1, 1), (0, 0)))
    running = jnp.zeros((frames * rows_here * cols_here, channels), jnp.float32)
    for tap_row in range(3):
        for tap_col in range(3):
            tap_index = 3 * tap_row + tap_col
            window = padded[
                :, tap_row : tap_row + rows_here, tap_col : tap_col + cols_here, :
            ].reshape(-1, channels)
            running = running + jnp.dot(
                window,
                weights[tap_index * channels : (tap_index + 1) * channels],
                preferred_element_type=jnp.float32,
            )
    return running.reshape(frames, rows_here, cols_here, channels)


def spatial_backward(activated, grad_out, weights):
    frames, rows_here, cols_here, channels = activated.shape
    pad_act = jnp.pad(activated, ((0, 0), (1, 1), (1, 1), (0, 0)))
    pad_grad = jnp.pad(grad_out, ((0, 0), (1, 1), (1, 1), (0, 0)))
    flat_grad = grad_out.reshape(-1, channels)
    running = jnp.zeros((frames * rows_here * cols_here, channels), jnp.float32)
    pieces = []
    for tap_row in range(3):
        for tap_col in range(3):
            tap_index = 3 * tap_row + tap_col
            block = weights[tap_index * channels : (tap_index + 1) * channels]
            window_grad = pad_grad[
                :, 2 - tap_row : 2 - tap_row + rows_here, 2 - tap_col : 2 - tap_col + cols_here, :
            ].reshape(-1, channels)
            running = running + jnp.dot(window_grad, block.T, preferred_element_type=jnp.float32)
            window_act = pad_act[
                :, tap_row : tap_row + rows_here, tap_col : tap_col + cols_here, :
            ].reshape(-1, channels)
            pieces.append(contract(window_act, flat_grad))
    return (
        running.reshape(frames, rows_here, cols_here, channels),
        jnp.concatenate(pieces, axis=0),
    )


def temporal_apply(extended, weights, frames):
    channels = extended.shape[-1]
    shape_out = (extended.shape[0], frames, extended.shape[2], channels)
    running = jnp.zeros((shape_out[0] * frames * shape_out[2], channels), jnp.float32)
    for time_delay in range(3):
        earlier = extended[:, 2 - time_delay : 2 - time_delay + frames].reshape(-1, channels)
        running = running + jnp.dot(
            earlier,
            weights[time_delay * channels : (time_delay + 1) * channels],
            preferred_element_type=jnp.float32,
        )
    return running.reshape(shape_out)


def temporal_adjoint(earlier_ext, later_ext, grad_rows, weights):
    frames = grad_rows.shape[1]
    channels = grad_rows.shape[-1]
    flat_grad = grad_rows.reshape(-1, channels)
    running = jnp.zeros(flat_grad.shape, jnp.float32)
    pieces = []
    for time_delay in range(3):
        block = weights[time_delay * channels : (time_delay + 1) * channels]
        later_rows = later_ext[:, time_delay : time_delay + frames].reshape(-1, channels)
        running = running + jnp.dot(later_rows, block.T, preferred_element_type=jnp.float32)
        earlier = earlier_ext[:, 2 - time_delay : 2 - time_delay + frames].reshape(-1, channels)
        pieces.append(contract(earlier, flat_grad))
    return (running.reshape(grad_rows.shape), jnp.concatenate(pieces, axis=0))


def local(latents, cotangent, norm_gain, norm_bias, w_spatial, w_temporal):
    clip_count, frames, rows_here, cols_here, channels = latents.shape
    per_group = channels // GROUPS
    cell_count = rows_here * cols_here
    spatial_full, temporal_full = (
        lax.all_gather(w_spatial, "dp", axis=0, tiled=True),
        lax.all_gather(w_temporal, "dp", axis=0, tiled=True),
    )
    widened = latents.astype(jnp.float32).reshape(
        clip_count, frames, rows_here, cols_here, GROUPS, per_group
    )
    group_sums = jnp.sum(widened, axis=(1, 2, 3, 5))
    squares = jnp.sum(widened * widened, axis=(1, 2, 3, 5))
    total_sums, total_squares = lax.psum((group_sums, squares), "wide")
    cells_count = lax.axis_size("wide") * frames * rows_here * cols_here * per_group
    group_mean = total_sums / cells_count
    variance = total_squares / cells_count - group_mean * group_mean
    inv_std = 1.0 / jnp.sqrt(variance + epsilon)
    mean_wide = group_mean[:, None, None, None, :, None]
    std_wide = inv_std[:, None, None, None, :, None]
    whitened = (widened - mean_wide) * std_wide
    flat_white = whitened.reshape(latents.shape)
    normed = flat_white * norm_gain + norm_bias
    sigmoid = jax.nn.sigmoid(normed)
    activated = (normed * sigmoid).astype(jnp.bfloat16)
    silu_slope = sigmoid * (1.0 + normed * (1.0 - sigmoid))
    stacked = activated.reshape(clip_count * frames, rows_here, cols_here, channels)
    spatial = (
        spatial_forward(stacked, spatial_full)
        .astype(jnp.bfloat16)
        .reshape(clip_count, frames, cell_count, channels)
    )
    grad_rows = cotangent.reshape(clip_count, frames, cell_count, channels)
    row_slab = lax.all_to_all(spatial, "wide", split_axis=2, concat_axis=1, tiled=True)
    extended = jnp.pad(row_slab, ((0, 0), (2, 0), (0, 0), (0, 0)))
    mixed_rows = temporal_apply(extended, temporal_full, row_slab.shape[1])
    returned = lax.all_to_all(
        mixed_rows.astype(jnp.bfloat16), "wide", split_axis=1, concat_axis=2, tiled=True
    ).astype(mixed_rows.dtype)
    grad_slab = lax.all_to_all(grad_rows, "wide", split_axis=2, concat_axis=1, tiled=True)
    earlier_ext = jnp.pad(row_slab, ((0, 0), (2, 0), (0, 0), (0, 0)))
    later_ext = jnp.pad(grad_slab, ((0, 0), (0, 2), (0, 0), (0, 0)))
    slab_wide, local_temporal = temporal_adjoint(earlier_ext, later_ext, grad_slab, temporal_full)
    grad_spatial_act = lax.all_to_all(
        slab_wide.astype(jnp.bfloat16), "wide", split_axis=1, concat_axis=2, tiled=True
    )
    block_out = (latents.astype(jnp.float32) + returned.reshape(latents.shape)).astype(jnp.bfloat16)
    grad_stack = grad_spatial_act.reshape(clip_count * frames, rows_here, cols_here, channels)
    grad_activated, local_spatial = spatial_backward(stacked, grad_stack, spatial_full)
    grad_normed = grad_activated.reshape(latents.shape) * silu_slope
    gain_term = jnp.sum(grad_normed * flat_white, axis=(0, 1, 2, 3))
    bias_term = jnp.sum(grad_normed, axis=(0, 1, 2, 3))
    local_norm = jnp.stack([gain_term, bias_term])
    grad_white = (grad_normed * norm_gain).reshape(widened.shape)
    mean_part = jnp.sum(grad_white, axis=(1, 2, 3, 5))
    cross_part = jnp.sum(grad_white * whitened, axis=(1, 2, 3, 5))
    mean_total, cross_total = lax.psum((mean_part, cross_part), "wide")
    grad_mean = mean_total / cells_count
    grad_cross = cross_total / cells_count
    inner = (
        grad_white
        - grad_mean[:, None, None, None, :, None]
        - whitened * grad_cross[:, None, None, None, :, None]
    ) * std_wide
    grad_latents = (cotangent.astype(jnp.float32) + inner.reshape(latents.shape)).astype(
        jnp.bfloat16
    )
    part_spatial, part_temporal, part_norm = (
        lax.psum_scatter(local_spatial, "wide", scatter_dimension=1, tiled=True),
        lax.psum_scatter(local_temporal, "wide", scatter_dimension=1, tiled=True),
        lax.psum_scatter(local_norm, "wide", scatter_dimension=1, tiled=True),
    )
    summed_spatial, summed_temporal = (
        lax.psum_scatter(
            part_spatial.astype(jnp.bfloat16), "dp", scatter_dimension=0, tiled=True
        ).astype(jnp.float32),
        lax.psum_scatter(
            part_temporal.astype(jnp.bfloat16), "dp", scatter_dimension=0, tiled=True
        ).astype(jnp.float32),
    )
    summed_norm = lax.psum(part_norm, "dp")
    all_cells = (
        clip_count * lax.axis_size("dp") * frames * lax.axis_size("wide") * rows_here * cols_here
    )
    grad_scale = 1.0 / math.sqrt(all_cells)
    return (
        block_out,
        grad_latents,
        summed_spatial * grad_scale,
        summed_temporal * grad_scale,
        summed_norm * grad_scale,
    )


def solution(mesh):
    return jax.shard_map(
        local,
        mesh=mesh,
        in_specs=(
            P("dp", "wide", None, None, None),
            P("dp", "wide", None, None, None),
            P(),
            P(),
            P("dp", None),
            P("dp", None),
        ),
        out_specs=(
            P("dp", "wide", None, None, None),
            P("dp", "wide", None, None, None),
            P("dp", "wide"),
            P("dp", "wide"),
            P(None, "wide"),
        ),
        check_vma=False,
    )
```

profile of v0, /device:TPU:8, one launch (start us, length us, event | category | flops | bytes accessed | tf_op | source)
XLA Modules:
  0.0 1140.6 jit_solution(14482897674854768501)
XLA Ops:
  7.9 1.7 copy.53
  9.6 16.2 %all-to-all-start.2 = ((bf16[1,2,128,256]{3,1,0,2:T(2,128)(2,1)}), bf16[1,2,128,256]{3,1,0,2:T(2,128)(2,1)S(1)}, u32[]{:S(2)}, u32[]{:S(2)}) async-start(bf16[1,2,128,256]{3,1,0,2:T(2,128)(2,1)} %bitcast.21), calls=%async_computation.2 | async-start | bytes 262144 | tf_op jit(solution)/shard_map/all_to_all | solution.py:128
  25.8 94.2 %all_gather.7 = bf16[768,256]{1,0:T(8,128)(2,1)S(1)} all-gather(bf16[96,256]{1,0:T(8,128)(2,1)} %param.11), channel_id=1, replica_groups=mesh['dp'=8,'wide'=64] {'dp'}, dimensions={0}, use_global_device_ids=true | all-gather | bytes 442368 | tf_op jit(solution)/shard_map/all_gather | solution.py:95
  122.5 17.6 %all-to-all-start.3 = ((bf16[1,128,2,256]{3,2,0,1:T(2,128)(2,1)}), bf16[1,128,2,256]{3,2,0,1:T(2,128)(2,1)S(1)}, u32[]{:S(2)}, u32[]{:S(2)}) async-start(bf16[1,128,2,256]{3,2,0,1:T(2,128)(2,1)} %bitcast.25), calls=%async_computation.3 | async-start | bytes 262144 | tf_op jit(solution)/shard_map/all_to_all | solution.py:132
  140.6 198.8 %all-reduce.8 = (f32[1,32]{1,0:T(1,128)S(1)}, f32[1,32]{1,0:T(1,128)S(1)}) all-reduce(f32[1,32]{1,0:T(1,128)S(1)} %bitcast.167, f32[1,32]{1,0:T(1,128)S(1)} %bitcast.166), channel_id=1, replica_groups=mesh['dp'=8,'wide'=64] {'wide'}, use_global_device_ids=true, to_apply=%region_5.6 | all-reduce | flops 64 | bytes 512 | tf_op jit(solution)/shard_map/psum | solution.py:102
  339.8 1.3 dynamic-slice
  343.1 1.2 fusion.53
  344.3 1.1 convolution_add_fusion.7
  349.4 0.9 convolution_dynamic-update-slice_fusion.8
  352.8 26.5 %all-to-all-start = ((bf16[1,2,128,256]{3,1,0,2:T(2,128)(2,1)}), bf16[1,2,128,256]{3,1,0,2:T(2,128)(2,1)S(1)}, u32[]{:S(2)}, u32[]{:S(2)}) async-start(bf16[1,2,128,256]{3,1,0,2:T(2,128)(2,1)} %copy.47), calls=%async_computation | async-start | bytes 262144 | tf_op jit(solution)/shard_map/all_to_all | solution.py:122
  379.3 0.9 convolution_dynamic-update-slice_fusion.7
  380.3 0.9 convolution_dynamic-update-slice_fusion.6
  381.2 0.9 convolution_dynamic-update-slice_fusion.5
  382.1 0.9 convolution_dynamic-update-slice_fusion.4
  383.1 0.9 convolution_dynamic-update-slice_fusion.3
  384.0 0.9 convolution_dynamic-update-slice_fusion.2
  384.9 0.9 convolution_dynamic-update-slice_fusion.1
  385.9 0.9 convolution_dynamic-update-slice_fusion
  386.8 6.0 all-to-all-done
  392.8 0.9 convolution_bitcast_fusion
  394.5 0.9 fusion.60
  395.6 0.9 fusion.61
  397.4 1.6 convert_element_type.106
  399.0 1.2 pad_maximum_fusion
  400.2 423.7 %all-reduce.10 = (f32[1,32]{1,0:T(1,128)}, f32[1,32]{1,0:T(1,128)}, bf16[2304,256]{1,0:T(8,128)(2,1)}, bf16[768,256]{1,0:T(8,128)(2,1)}, f32[2,256]{1,0:T(2,128)}) all-reduce(f32[1,32]{1,0:T(1,128)} %bitcast.164, f32[1,32]{1,0:T(1,128)} %bitcast.165, f32[2304,256]{1,0:T(8,128)S(1)} %copy-done.1, ...), channel_id=1, replica_groups=mesh['dp'=8,'wide'=64] {'wide'}, use_global_device_ids=true, to_apply=%region_11.12 | all-reduce | flops 787008 | bytes 4723200 | tf_op jit(solution)/shard_map/psum | solution.py:145
  824.6 44.1 %all-to-all-start.1 = ((bf16[1,128,2,256]{3,2,0,1:T(2,128)(2,1)}), bf16[1,128,2,256]{3,2,0,1:T(2,128)(2,1)S(1)}, u32[]{:S(2)}, u32[]{:S(2)}) async-start(bf16[1,128,2,256]{3,2,0,1:T(2,128)(2,1)} %bitcast.149), calls=%async_computation.1 | async-start | bytes 262144 | tf_op jit(solution)/shard_map/all_to_all | solution.py:125
  868.8 44.0 %psum.39 = f32[2,4]{1,0:T(2,128)S(1)} all-reduce(f32[2,4]{1,0:T(2,128)S(1)} %constant_dynamic-slice_fusion), channel_id=1, replica_groups=mesh['dp'=8,'wide'=64] {'dp'}, use_global_device_ids=true, to_apply=%region_19.20 | all-reduce | flops 8 | bytes 64 | tf_op jit(solution)/shard_map/psum | solution.py:169
  913.4 1.7 dynamic-slice_convert_fusion.1
  915.1 2.1 dynamic-slice_convert_fusion
  918.0 103.3 %reduce-scatter.8.cloned.1.call-done = bf16[96,4]{1,0:T(8,128)(2,1)} async-done(((bf16[768,4]{1,0:T(8,128)(2,1)}), bf16[96,4]{1,0:T(8,128)(2,1)}) %reduce-scatter.8.cloned.1.call-update) | async-done | bytes 784 | tf_op jit(solution)/shard_map/reduce_scatter | solution.py:165
  1022.7 108.6 %reduce-scatter.6.cloned.1.call-done = bf16[288,4]{1,0:T(8,128)(2,1)} async-done(((bf16[2304,4]{1,0:T(8,128)(2,1)}), bf16[288,4]{1,0:T(8,128)(2,1)}) %reduce-scatter.6.cloned.1.call-update) | async-done | bytes 2320 | tf_op jit(solution)/shard_map/reduce_scatter | solution.py:162
  1131.3 0.9 convert_multiply_fusion.1
  (113 shorter events, 18.6 us)
Async XLA Ops:
  7.2 335.9 %all-gather.2.cloned.1.call-start = ((), (), s32[]{:S(2)}) async-start(), calls=%async_computation.6 | async-start | bytes 1327104 | tf_op jit(solution)/shard_map/all_gather | solution.py:94
  9.6 110.4 %all-to-all-start.2 = ((bf16[1,2,128,256]{3,1,0,2:T(2,128)(2,1)}), bf16[1,2,128,256]{3,1,0,2:T(2,128)(2,1)S(1)}, u32[]{:S(2)}, u32[]{:S(2)}) async-start(bf16[1,2,128,256]{3,1,0,2:T(2,128)(2,1)} %bitcast.21), calls=%async_computation.2 | async-start | bytes 262144 | tf_op jit(solution)/shard_map/all_to_all | solution.py:128
  120.0 0.7 copy-start.4
  121.1 19.0 %copy-start.2 = (bf16[1,2,8,16,256]{4,3,2,1,0:T(8,128)(2,1)S(1)}, bf16[1,2,8,16,256]{4,3,2,1,0:T(8,128)(2,1)}, u32[]{:S(2)}) copy-start(bf16[1,2,8,16,256]{4,3,2,1,0:T(8,128)(2,1)} %param.6) | copy-start | bytes 393220
  122.5 219.2 %all-to-all-start.3 = ((bf16[1,128,2,256]{3,2,0,1:T(2,128)(2,1)}), bf16[1,128,2,256]{3,2,0,1:T(2,128)(2,1)S(1)}, u32[]{:S(2)}, u32[]{:S(2)}) async-start(bf16[1,128,2,256]{3,2,0,1:T(2,128)(2,1)} %bitcast.25), calls=%async_computation.3 | async-start | bytes 262144 | tf_op jit(solution)/shard_map/all_to_all | solution.py:132
  343.1 2.4 copy-start
  346.3 0.7 copy-start.6
  346.3 0.7 copy-start.9
  352.8 40.0 %all-to-all-start = ((bf16[1,2,128,256]{3,1,0,2:T(2,128)(2,1)}), bf16[1,2,128,256]{3,1,0,2:T(2,128)(2,1)S(1)}, u32[]{:S(2)}, u32[]{:S(2)}) async-start(bf16[1,2,128,256]{3,1,0,2:T(2,128)(2,1)} %copy.47), calls=%async_computation | async-start | bytes 262144 | tf_op jit(solution)/shard_map/all_to_all | solution.py:122
  383.1 3.8 copy-start.7
  383.1 3.8 copy-start.8
  383.1 9.8 copy-start.5
  396.6 3.6 copy-start.1
  823.9 93.4 %copy-start.10 = (f32[1,32]{1,0:T(1,128)S(1)}, f32[1,32]{1,0:T(1,128)}, u32[]{:S(2)}) copy-start(f32[1,32]{1,0:T(1,128)} %get-tuple-element.31) | copy-start | bytes 388
  823.9 93.4 %copy-start.11 = (f32[1,32]{1,0:T(1,128)S(1)}, f32[1,32]{1,0:T(1,128)}, u32[]{:S(2)}) copy-start(f32[1,32]{1,0:T(1,128)} %get-tuple-element.32) | copy-start | bytes 388
  824.6 308.3 %all-to-all-start.1 = ((bf16[1,128,2,256]{3,2,0,1:T(2,128)(2,1)}), bf16[1,128,2,256]{3,2,0,1:T(2,128)(2,1)S(1)}, u32[]{:S(2)}, u32[]{:S(2)}) async-start(bf16[1,128,2,256]{3,2,0,1:T(2,128)(2,1)} %bitcast.149), calls=%async_computation.1 | async-start | bytes 262144 | tf_op jit(solution)/shard_map/all_to_all | solution.py:125
  868.8 152.5 %reduce-scatter.8.cloned.1.call-start = ((), (), s32[]{:S(2)}) async-start(), calls=%async_computation.8 | async-start | bytes 221184 | tf_op jit(solution)/shard_map/reduce_scatter | solution.py:165
  917.2 214.1 %reduce-scatter.6.cloned.1.call-start = ((), (), s32[]{:S(2)}) async-start(), calls=%async_computation.7 | async-start | bytes 663552 | tf_op jit(solution)/shard_map/reduce_scatter | solution.py:162
  917.7 215.6 %copy-start.3 = (bf16[1,2,8,16,256]{4,3,2,1,0:T(8,128)(2,1)S(1)}, bf16[1,2,8,16,256]{4,3,2,1,0:T(8,128)(2,1)}, u32[]{:S(2)}) copy-start(bf16[1,2,8,16,256]{4,3,2,1,0:T(8,128)(2,1)} %param.7) | copy-start | bytes 393220
Sparse Core Ops, SparseCore 0:
  11.2 113.4 all-gather.1
  917.4 103.9 reduce-scatter.7
  1026.5 104.8 reduce-scatter.5
where the time goes:
time: 1140 us
  blocking collectives  761 us (67%)
  waiting for transfers between devices  219 us (19%)
  starting transfers between devices  105 us (9%)
  matrix products  18.6 us (2%)
  local copies, waits for them, and re-layouts  16.2 us (1%)
  between operations  15 us (1%)
    psum x1, blocking collectives, local(): mean_total, cross_total = lax.psum((mean_part, cross_part), 'wide')  424 us
    psum x1, blocking collectives, local(): total_sums, total_squares = lax.psum((group_sums, squares), 'wide')  199 us
    reduce_scatter x1, waiting for transfers between devices, local(): lax.psum_scatter(part_spatial.astype(jnp.bfloat16), 'dp', scatter_dimensi...  109 us
    reduce_scatter x1, waiting for transfers between devices, local(): lax.psum_scatter(part_temporal.astype(jnp.bfloat16), 'dp', scatter_dimens...  103 us
    all_gather x1, blocking collectives, local(): lax.all_gather(w_temporal, 'dp', axis=0, tiled=True)  94.2 us
    all_to_all x1, starting transfers between devices, local(): lax.all_to_all(mixed_rows.astype(jnp.bfloat16), 'wide', split_axis=1, con...  44.1 us
    psum x1, blocking collectives, local(): summed_norm = lax.psum(part_norm, 'dp')  44 us
    all_to_all x1, starting transfers between devices, local(): lax.all_to_all(spatial, 'wide', split_axis=2, concat_axis=1, tiled=True)  26.5 us
  transfers between devices with their start and end apart: 7, of which 3 were waited for; matrix products, arithmetic and copies ran while one was open for 2% of the time, Pallas kernels for 0%

commit v1 on v0

--- a/solution.py
+++ b/solution.py
@@ -92,7 +92,9 @@
     cell_count = rows_here * cols_here
     spatial_full, temporal_full = (
         lax.all_gather(w_spatial, "dp", axis=0, tiled=True),
-        lax.all_gather(w_temporal, "dp", axis=0, tiled=True),
+        jnp.concatenate(
+            lax.all_to_all(jnp.stack([w_temporal] * lax.axis_size("dp")), "dp", 0, 0), axis=0
+        ),
     )
     widened = latents.astype(jnp.float32).reshape(
         clip_count, frames, rows_here, cols_here, GROUPS, per_group

time: 1140 us -> 1090 us (0.956)
  blocking collectives: 761 us -> 701 us
  waiting for transfers between devices: 219 us -> 236 us
  starting transfers between devices: 105 us -> 91.3 us
    all_gather x1 -> x0, blocking collectives: 94.2 us -> none  [local(): lax.all_gather(w_temporal, 'dp', axis=0, tiled=True)]
    all_to_all x0 -> x1, blocking collectives: none -> 29.5 us  [local(): lax.all_to_all(grad_rows, 'wide', split_axis=2, concat_axis=1, tiled=True)]
    all_to_all x1, waiting for transfers between devices: 0.01 us -> 16.5 us  [local(): lax.all_to_all(jnp.stack([w_temporal] * lax.axis_size('dp')), 'dp', 0, 0)]
  transfers between devices with their start and end apart: 7 -> 7, of which waited for: 3 -> 4; matrix products, arithmetic and copies ran while one was open for 2% -> 2% of each run, Pallas kernels for 0% -> 0%
where the time goes in v1:
time: 1090 us; the launch traced here: 1080 us
  blocking collectives  701 us (64%)
  waiting for transfers between devices  236 us (22%)
  starting transfers between devices  91.3 us (8%)
  matrix products  18.6 us (2%)
  local copies, waits for them, and re-layouts  16.6 us (2%)
  between operations  15 us (1%)
    psum x1, blocking collectives, local(): mean_total, cross_total = lax.psum((mean_part, cross_part), 'wide')  424 us
    psum x1, blocking collectives, local(): total_sums, total_squares = lax.psum((group_sums, squares), 'wide')  210 us
    reduce_scatter x1, waiting for transfers between devices, local(): lax.psum_scatter(part_spatial.astype(jnp.bfloat16), 'dp', scatter_dimensi...  109 us
    reduce_scatter x1, waiting for transfers between devices, local(): lax.psum_scatter(part_temporal.astype(jnp.bfloat16), 'dp', scatter_dimens...  104 us
    all_to_all x1, starting transfers between devices, local(): lax.all_to_all(mixed_rows.astype(jnp.bfloat16), 'wide', split_axis=1, con...  44.1 us
    psum x1, blocking collectives, local(): summed_norm = lax.psum(part_norm, 'dp')  38.5 us
    all_to_all x1, blocking collectives, local(): lax.all_to_all(grad_rows, 'wide', split_axis=2, concat_axis=1, tiled=True)  29.5 us
  transfers between devices with their start and end apart: 7, of which 4 were waited for; matrix products, arithmetic and copies ran while one was open for 2% of the time, Pallas kernels for 0%

profile of v1, /device:TPU:8, one launch (start us, length us, event | category | flops | bytes accessed | tf_op | source)
XLA Modules:
  0.0 1084.9 jit_solution(2755297312431815587)
XLA Ops:
  7.2 1.0 copy.53
  8.2 29.5 %all_to_all.65 = bf16[1,2,128,256]{3,1,0,2:T(2,128)(2,1)S(1)} all-to-all(bf16[1,2,128,256]{3,1,0,2:T(2,128)(2,1)S(1)} %bitcast.160), channel_id=1, replica_groups=mesh['dp'=8,'wide'=64] {'wide'}, dimensions={2} | all-to-all | bytes 262144 | tf_op jit(solution)/shard_map/all_to_all | solution.py:130
  37.7 1.6 stack.8
  39.3 10.0 all-to-all-start.1
  50.6 16.5 %all-to-all-done.1 = bf16[8,96,256]{2,1,0:T(8,128)(2,1)S(1)} async-done(((bf16[8,96,256]{2,1,0:T(8,128)(2,1)}), bf16[8,96,256]{2,1,0:T(8,128)(2,1)S(1)}, u32[]{:S(2)}, u32[]{:S(2)}) %all-to-all-start.1) | async-done | bytes 393248 | tf_op jit(solution)/shard_map/all_to_all | solution.py:96
  68.5 18.6 %all-to-all-start.4 = ((bf16[1,128,2,256]{3,2,0,1:T(2,128)(2,1)}), bf16[1,128,2,256]{3,2,0,1:T(2,128)(2,1)S(1)}, u32[]{:S(2)}, u32[]{:S(2)}) async-start(bf16[1,128,2,256]{3,2,0,1:T(2,128)(2,1)} %bitcast.26), calls=%async_computation.4 | async-start | bytes 262144 | tf_op jit(solution)/shard_map/all_to_all | solution.py:134
  87.6 209.5 %all-reduce.8 = (f32[1,32]{1,0:T(1,128)S(1)}, f32[1,32]{1,0:T(1,128)S(1)}) all-reduce(f32[1,32]{1,0:T(1,128)S(1)} %bitcast.175, f32[1,32]{1,0:T(1,128)S(1)} %bitcast.174), channel_id=1, replica_groups=mesh['dp'=8,'wide'=64] {'wide'}, use_global_device_ids=true, to_apply=%region_5.6 | all-reduce | flops 64 | bytes 512 | tf_op jit(solution)/shard_map/psum | solution.py:104
  297.5 1.3 dynamic-slice
  300.8 1.2 fusion.53
  302.0 1.1 convolution_add_fusion.7
  310.5 18.4 %all-to-all-start = ((bf16[1,2,128,256]{3,1,0,2:T(2,128)(2,1)}), bf16[1,2,128,256]{3,1,0,2:T(2,128)(2,1)S(1)}, u32[]{:S(2)}, u32[]{:S(2)}) async-start(bf16[1,2,128,256]{3,1,0,2:T(2,128)(2,1)} %copy.47), calls=%async_computation | async-start | bytes 262144 | tf_op jit(solution)/shard_map/all_to_all | solution.py:124
  329.0 0.9 convolution_dynamic-update-slice_fusion.7
  329.9 0.9 convolution_dynamic-update-slice_fusion.6
  330.8 0.9 convolution_dynamic-update-slice_fusion.5
  331.7 0.9 convolution_dynamic-update-slice_fusion.4
  332.7 0.9 convolution_dynamic-update-slice_fusion.3
  333.6 0.9 convolution_dynamic-update-slice_fusion.2
  334.6 0.9 convolution_dynamic-update-slice_fusion.1
  335.5 0.9 convolution_dynamic-update-slice_fusion
  336.5 6.0 all-to-all-done
  342.5 0.9 convolution_bitcast_fusion
  344.1 0.9 fusion.60
  345.2 0.9 fusion.61
  347.0 1.6 convert_element_type.106
  348.6 1.2 pad_maximum_fusion
  349.8 423.6 %all-reduce.10 = (f32[1,32]{1,0:T(1,128)}, f32[1,32]{1,0:T(1,128)}, bf16[2304,256]{1,0:T(8,128)(2,1)}, bf16[768,256]{1,0:T(8,128)(2,1)}, f32[2,256]{1,0:T(2,128)}) all-reduce(f32[1,32]{1,0:T(1,128)} %bitcast.172, f32[1,32]{1,0:T(1,128)} %bitcast.173, f32[2304,256]{1,0:T(8,128)S(1)} %copy-done.1, ...), channel_id=1, replica_groups=mesh['dp'=8,'wide'=64] {'wide'}, use_global_device_ids=true, to_apply=%region_11.12 | all-reduce | flops 787008 | bytes 4723200 | tf_op jit(solution)/shard_map/psum | solution.py:147
  774.2 44.1 %all-to-all-start.2 = ((bf16[1,128,2,256]{3,2,0,1:T(2,128)(2,1)}), bf16[1,128,2,256]{3,2,0,1:T(2,128)(2,1)S(1)}, u32[]{:S(2)}, u32[]{:S(2)}) async-start(bf16[1,128,2,256]{3,2,0,1:T(2,128)(2,1)} %bitcast.156), calls=%async_computation.2 | async-start | bytes 262144 | tf_op jit(solution)/shard_map/all_to_all | solution.py:127
  818.4 38.5 %psum.39 = f32[2,4]{1,0:T(2,128)S(1)} all-reduce(f32[2,4]{1,0:T(2,128)S(1)} %constant_dynamic-slice_fusion), channel_id=1, replica_groups=mesh['dp'=8,'wide'=64] {'dp'}, use_global_device_ids=true, to_apply=%region_19.20 | all-reduce | flops 8 | bytes 64 | tf_op jit(solution)/shard_map/psum | solution.py:171
  857.4 1.7 dynamic-slice_convert_fusion.1
  859.2 2.1 dynamic-slice_convert_fusion
  862.1 103.6 %reduce-scatter.8.cloned.1.call-done = bf16[96,4]{1,0:T(8,128)(2,1)} async-done(((bf16[768,4]{1,0:T(8,128)(2,1)}), bf16[96,4]{1,0:T(8,128)(2,1)}) %reduce-scatter.8.cloned.1.call-update) | async-done | bytes 784 | tf_op jit(solution)/shard_map/reduce_scatter | solution.py:167
  967.0 108.6 %reduce-scatter.6.cloned.1.call-done = bf16[288,4]{1,0:T(8,128)(2,1)} async-done(((bf16[2304,4]{1,0:T(8,128)(2,1)}), bf16[288,4]{1,0:T(8,128)(2,1)}) %reduce-scatter.6.cloned.1.call-update) | async-done | bytes 2320 | tf_op jit(solution)/shard_map/reduce_scatter | solution.py:164
  (114 shorter events, 19.8 us)
Async XLA Ops:
  37.7 12.4 %copy-start.4 = (bf16[1,2,128,256]{3,1,0,2:T(2,128)(2,1)}, bf16[1,2,128,256]{3,1,0,2:T(2,128)(2,1)S(1)}, u32[]{:S(2)}) copy-start(bf16[1,2,128,256]{3,1,0,2:T(2,128)(2,1)S(1)} %all_to_all.65) | copy-start | bytes 393220
  39.3 27.8 %all-to-all-start.1 = ((bf16[8,96,256]{2,1,0:T(8,128)(2,1)}), bf16[8,96,256]{2,1,0:T(8,128)(2,1)S(1)}, u32[]{:S(2)}, u32[]{:S(2)}) async-start(bf16[8,96,256]{2,1,0:T(8,128)(2,1)} %stack.8), calls=%async_computation.1 | async-start | bytes 786432 | tf_op jit(solution)/shard_map/all_to_all | solution.py:96
  49.3 251.4 %all-gather.2.cloned.1.call-start = ((), (), s32[]{:S(2)}) async-start(), calls=%async_computation.7 | async-start | bytes 1327104 | tf_op jit(solution)/shard_map/all_gather | solution.py:94
  67.1 20.0 %copy-start.2 = (bf16[1,2,8,16,256]{4,3,2,1,0:T(8,128)(2,1)S(1)}, bf16[1,2,8,16,256]{4,3,2,1,0:T(8,128)(2,1)}, u32[]{:S(2)}) copy-start(bf16[1,2,8,16,256]{4,3,2,1,0:T(8,128)(2,1)} %param.6) | copy-start | bytes 393220
  68.5 230.9 %all-to-all-start.4 = ((bf16[1,128,2,256]{3,2,0,1:T(2,128)(2,1)}), bf16[1,128,2,256]{3,2,0,1:T(2,128)(2,1)S(1)}, u32[]{:S(2)}, u32[]{:S(2)}) async-start(bf16[1,128,2,256]{3,2,0,1:T(2,128)(2,1)} %bitcast.26), calls=%async_computation.4 | async-start | bytes 262144 | tf_op jit(solution)/shard_map/all_to_all | solution.py:134
  300.8 2.4 copy-start
  304.0 0.7 copy-start.6
  304.1 0.7 copy-start.9
  310.5 31.9 %all-to-all-start = ((bf16[1,2,128,256]{3,1,0,2:T(2,128)(2,1)}), bf16[1,2,128,256]{3,1,0,2:T(2,128)(2,1)S(1)}, u32[]{:S(2)}, u32[]{:S(2)}) async-start(bf16[1,2,128,256]{3,1,0,2:T(2,128)(2,1)} %copy.47), calls=%async_computation | async-start | bytes 262144 | tf_op jit(solution)/shard_map/all_to_all | solution.py:124
  332.7 3.8 copy-start.7
  332.7 3.8 copy-start.8
  332.7 9.8 copy-start.5
  346.2 3.6 copy-start.1
  773.4 87.9 %copy-start.10 = (f32[1,32]{1,0:T(1,128)S(1)}, f32[1,32]{1,0:T(1,128)}, u32[]{:S(2)}) copy-start(f32[1,32]{1,0:T(1,128)} %get-tuple-element.31) | copy-start | bytes 388
  773.4 87.9 %copy-start.11 = (f32[1,32]{1,0:T(1,128)S(1)}, f32[1,32]{1,0:T(1,128)}, u32[]{:S(2)}) copy-start(f32[1,32]{1,0:T(1,128)} %get-tuple-element.32) | copy-start | bytes 388
  774.2 303.0 %all-to-all-start.2 = ((bf16[1,128,2,256]{3,2,0,1:T(2,128)(2,1)}), bf16[1,128,2,256]{3,2,0,1:T(2,128)(2,1)S(1)}, u32[]{:S(2)}, u32[]{:S(2)}) async-start(bf16[1,128,2,256]{3,2,0,1:T(2,128)(2,1)} %bitcast.156), calls=%async_computation.2 | async-start | bytes 262144 | tf_op jit(solution)/shard_map/all_to_all | solution.py:127
  818.3 147.3 %reduce-scatter.8.cloned.1.call-start = ((), (), s32[]{:S(2)}) async-start(), calls=%async_computation.9 | async-start | bytes 221184 | tf_op jit(solution)/shard_map/reduce_scatter | solution.py:167
  861.3 214.3 %reduce-scatter.6.cloned.1.call-start = ((), (), s32[]{:S(2)}) async-start(), calls=%async_computation.8 | async-start | bytes 663552 | tf_op jit(solution)/shard_map/reduce_scatter | solution.py:164
  861.7 215.8 %copy-start.3 = (bf16[1,2,8,16,256]{4,3,2,1,0:T(8,128)(2,1)S(1)}, bf16[1,2,8,16,256]{4,3,2,1,0:T(8,128)(2,1)}, u32[]{:S(2)}) copy-start(bf16[1,2,8,16,256]{4,3,2,1,0:T(8,128)(2,1)} %param.7) | copy-start | bytes 393220
Sparse Core Ops, SparseCore 0:
  53.4 95.4 all-gather.1
  861.4 104.1 reduce-scatter.7
  970.8 104.8 reduce-scatter.5
